TPU v7x, 32 devices: a whole 2x2x4 slice. The times are simulated.
32 devices in a mesh: row: 4 (over y, x), col: 8 (over z, core).
Axes of the slice: x: 2, y: 2, z: 4, core: 2. Of those that a mesh axis runs over, the one named last changes fastest.
Arguments:
- hist_corr: float32 [16384, 16384], P('row', 'col'), may hold values from -1 to 1
- hist_resp: float32 [16384, 16384], P('row', 'col'), may hold values from -1 to 1, as said below
- row_corr: float32 [128, 16384], P(None, 'col'), may hold values from -1 to 1
- row_resp: float32 [128, 16384], P(None, 'col'), may hold values from -1 to 1
Outputs:
- final_corr: float32 [128, 16384], P(None, 'col')
- final_resp: float32 [128, 16384], P(None, 'col')
Inputs may be any that keep to these rules, and one draw needn't show every extreme that they name: hist_resp[s, u] is 0 where u > s and 1 where u == s.
All inputs are finite; a program needn't handle non-finite values.
Results may differ from a plain program's by a relative error of at most 0.00015.
Values sent between devices are 32-bit elements; how exact they have to be, the bound alone decides.
A program may use at most 128 MiB of HBM per device.

v0:
```python
import functools
import math

import jax
import jax.numpy as jnp
from jax import lax
from jax.experimental import pallas as pl
from jax.experimental.pallas import tpu as pltpu
from jax.sharding import PartitionSpec as P

BLOCKS = 4
STEP = 0.2
WARMTH = 0.6


def plain_body(hist_corr, hist_resp, row_corr, row_resp):
    rows = lax.axis_size("row")
    span = row_corr.shape[0] // rows
    coef = 1.0 / math.sqrt(hist_corr.shape[0] * rows)
    start = lax.axis_index("row") * span
    corr = lax.dynamic_slice_in_dim(row_corr, start, span, 0)
    resp = lax.dynamic_slice_in_dim(row_resp, start, span, 0)

    def dot(a, b, dims):
        return lax.dot_general(
            a, b, (dims, ((), ())), precision=lax.Precision.HIGH, preferred_element_type=jnp.float32
        )

    for _ in range(BLOCKS):
        energy = 3.0 * corr * resp
        slope = 1.5 * corr * corr
        mult = lax.psum(jnp.sum(energy * corr + slope * resp, axis=1), "col")
        full = lax.all_gather(corr, "row", axis=0, tiled=True)
        wide = lax.all_gather(energy, "col", axis=1, tiled=True)
        energy_rows = lax.all_to_all(wide, "row", split_axis=1, concat_axis=0, tiled=True)
        part_cross = dot(1.5 * full * full, hist_resp, ((1,), (1,)))
        turned = lax.all_to_all(part_cross, "row", split_axis=0, concat_axis=1, tiled=True)
        cross = lax.psum_scatter(turned, "col", scatter_dimension=1, tiled=True)
        part_corr = dot(energy_rows, hist_corr, ((1,), (0,)))
        part_resp = dot(energy_rows, hist_resp, ((1,), (0,)))
        mem_corr = lax.psum_scatter(part_corr, "row", scatter_dimension=0, tiled=True)
        mem_resp = lax.psum_scatter(part_resp, "row", scatter_dimension=0, tiled=True)
        scalar = WARMTH + coef * mult[:, None]
        next_corr = corr + STEP * (coef * (mem_corr + cross) - scalar * corr)
        resp = resp + STEP * (coef * mem_resp - scalar * resp)
        corr = next_corr
    return (
        lax.all_gather(corr, "row", axis=0, tiled=True),
        lax.all_gather(resp, "row", axis=0, tiled=True),
    )


MESH = pl.DeviceIdType.MESH
F32 = jnp.float32


SLOTS = 3
BF16 = jnp.bfloat16


def split(x):
    hi = x.astype(BF16)
    return hi, (x - hi.astype(F32)).astype(BF16)


def block_kernel(last, coef, R, Z, hc, hr, c_prev, c_in, r_in, *refs):
    refs = list(refs)
    take = lambda n: [refs.pop(0) for _ in range(n)]
    if last:
        c_full, r_full = take(2)
    else:
        c_out, r_out, c_full = take(3)
    tiles, xp, acc, e_rows, estack, dstack = take(6)
    xbuf, xsum, xin, up, mrecv, racc, csrc, eall, mbuf = take(9)
    (tsem,) = take(1)
    xs, xr, xis, xir, ups, upr, ms, mrs, cs, crs = take(10)
    eus, eur, eds, edr, eis, eir, ps, pr, mus, mur = take(10)
    assert not refs
    T, U = c_in.shape
    M = R * T
    N = 2 * Z
    CH = tiles.shape[1]
    per = U // CH
    count = 2 * per
    r, c = lax.axis_index("row"), lax.axis_index("col")
    z = lax.div(c, 2)
    k = c - 2 * z
    partner = 2 * z + 1 - k
    rows = [lax.rem(r + d, R) for d in range(1, R)]
    cols = [lax.rem(c + d, N) for d in range(1, N)]
    low = z <= r

    def rc(src, dst, ss, rs, row, col):
        return pltpu.make_async_remote_copy(
            src_ref=src, dst_ref=dst, send_sem=ss, recv_sem=rs, device_id=(row, col), device_id_type=MESH
        )

    def at_row(q):
        return pl.ds(pl.multiple_of(q * T, T), T)

    def half(h):
        return pl.ds(pl.multiple_of(h * U, U), U)

    def x_start(i):
        side = 1 - k if i < per else k
        return pl.multiple_of(side * U + (i % per) * CH, CH)

    def tile_copy(n):
        kind, i = divmod(n, count)
        start = x_start(i) if kind == 0 else i * CH
        src = hc if kind == 1 else hr
        return pltpu.make_async_copy(src.at[pl.ds(start, CH)], tiles.at[n % SLOTS], tsem.at[n % SLOTS])

    tile_copy(0).start()
    tile_copy(1).start()

    barrier = pltpu.get_barrier_semaphore()
    for q in rows:
        pl.semaphore_signal(barrier, inc=1, device_id=(q, c), device_id_type=MESH)
    for q in cols:
        pl.semaphore_signal(barrier, inc=1, device_id=(r, q), device_id_type=MESH)

    energy = 3.0 * c_in[...] * r_in[...]
    eall[z] = energy
    terms = energy * c_in[...] + 1.5 * c_in[...] * c_in[...] * r_in[...]
    part = terms[:, :128]
    for i in range(1, U // 128):
        part = part + terms[:, i * 128 : (i + 1) * 128]
    mbuf[c] = part
    pl.semaphore_wait(barrier, R - 1 + N - 1)

    def flow(p, step):
        ss, rs = (eus, eur) if step > 0 else (eds, edr)
        return rc(eall.at[p], eall.at[p], ss.at[p], rs.at[p], r, c + step)

    def inplane(d, p):
        return rc(eall.at[p], e_rows.at[at_row(r), half(k)], eis.at[d], eir.at[d], p, c)

    def turn(p):
        @pl.when(p == r)
        def _():
            e_rows[at_row(r), half(k)] = eall[p]

        @pl.when(p != r)
        def _():
            inplane(lax.rem(p - r + R, R) - 1, p).start()

    pair = rc(e_rows.at[:, half(k)], e_rows.at[:, half(k)], ps, pr, r, partner)

    def share(h):
        @pl.when(jnp.logical_or(z - r == h, r - z == h))
        def _():
            for d in range(R - 1):
                inplane(d, rows[d]).wait_recv()
            pair.start()

    def hop(h):
        @pl.when(z - h >= 0)
        def _():
            flow(z - h, 2).wait_recv()

            @pl.when(z < Z - 1)
            def _():
                flow(z - h, 2).start()

        @pl.when(z + h <= Z - 1)
        def _():
            flow(z + h, -2).wait_recv()

            @pl.when(z > 0)
            def _():
                flow(z + h, -2).start()

            turn(z + h)

        @pl.when(z - h >= 0)
        def _():
            turn(z - h)

        share(h - 1)

    def mucopy(d):
        return rc(mbuf.at[c], mbuf.at[c], mus.at[d], mur.at[d], r, cols[d])

    @pl.when(z < Z - 1)
    def _():
        flow(z, 2).start()

    @pl.when(z > 0)
    def _():
        flow(z, -2).start()

    turn(z)
    for d in range(N - 1):
        mucopy(d).start()

    xcopy = rc(xp.at[:, half(1 - k)], xbuf, xs, xr, r, partner)

    def mcopy(d, which):
        q = rows[d]
        return rc(acc.at[which, at_row(q)], mrecv.at[d, which], ms.at[d, which], mrs.at[d, which], q, c)

    def xcopy2(d):
        return rc(xsum.at[at_row(rows[d])], xin.at[r], xis.at[d], xir.at[d], rows[d], c)

    def upcopy(j, col):
        return rc(xin.at[j], up.at[j], ups.at[j], upr.at[j], r, col)

    def x_begin():
        @pl.when(low)
        def _():
            xcopy.start()

    def x_turn():
        @pl.when(low)
        def _():
            xcopy.wait()
            xsum[...] = xp[:, half(k)] + xbuf[...]
            xin[r] = xsum[at_row(r)]
            for d in range(R - 1):
                xcopy2(d).start()

    def climb(zz, j):
        @pl.when(z == zz)
        def _():
            @pl.when(r != j)
            def _():
                d = lax.rem(r - j + R, R)
                rc(xin.at[j], xin.at[j], xis.at[d - 1], xir.at[d - 1], j, c).wait_recv()

            if zz > 0:
                upcopy(j, c - 2).wait_recv()
                xin[j] = xin[j] + up[j]
            if zz < j:
                upcopy(j, c + 2).start()

    def e_ready():
        share(Z - 1)
        pair.wait()

        @pl.loop(0, M // 32)
        def _(i):
            rows32 = pl.ds(pl.multiple_of(i * 32, 32), 32)
            hi, lo = split(e_rows[rows32, :])
            estack[rows32, :] = hi
            estack[pl.ds(pl.multiple_of(M + i * 32, 32), 32), :] = lo

    def m_send(which):
        for d in range(R - 1):
            if which == 0:
                mcopy(d, 0).start()
            else:
                @pl.when(low)
                def _():
                    mcopy(d, 1).start()

    def x_tile(i, slot):
        where = pl.ds(x_start(i), CH)
        xp[:, where] = jnp.zeros((M, CH), F32)

        @pl.loop(0, per)
        def _(b):
            at = pl.ds(pl.multiple_of(b * CH, CH), CH)
            hi, lo = split(tiles[slot, :, at])
            both = dstack[:, at]
            dims = (((1,), (1,)), ((), ()))
            p = lax.dot_general(both, hi, dims, preferred_element_type=F32)
            q = lax.dot_general(both[:M], lo, dims, preferred_element_type=F32)
            xp[:, where] += p[:M] + p[M:] + q

    def m_tile(which, i, slot):
        @pl.loop(0, per)
        def _(b):
            at = pl.ds(pl.multiple_of(b * CH, CH), CH)
            hi, lo = split(tiles[slot, :, at])
            both = estack[:, i * CH : (i + 1) * CH]
            dims = (((1,), (0,)), ((), ()))
            p = lax.dot_general(both, hi, dims, preferred_element_type=F32)
            q = lax.dot_general(both[:M], lo, dims, preferred_element_type=F32)
            out = p[:M] + p[M:] + q
            if i == 0:
                acc[which, :, at] = out
            else:
                acc[which, :, at] += out

    @pl.loop(0, M // 32)
    def _(i):
        rows32 = pl.ds(pl.multiple_of(i * 32, 32), 32)
        old = c_prev[rows32, :]
        hi, lo = split(1.5 * old * old)
        dstack[rows32, :] = hi
        dstack[pl.ds(pl.multiple_of(M + i * 32, 32), 32), :] = lo

    hooks = {}

    def hook(n, f, *args):
        hooks.setdefault(n, []).append((f, args))

    hook(per - 1, x_begin)
    for h in range(1, Z):
        hook(min((h * count) // Z - 1 + (h > 2), count - 1), hop, h)
    hook(count - 1, e_ready)
    hook(count, x_turn)
    for zz in range(Z):
        for j in reversed(range(zz, Z)):
            hook(count + 2 + 2 * zz + (Z - 1 - j), climb, zz, j)
    hook(2 * count - 1, m_send, 0)
    hook(3 * count - 1, m_send, 1)
    for n in range(3 * count):
        if n + 2 < 3 * count:
            tile_copy(n + 2).start()
        tile_copy(n).wait()
        kind, i = divmod(n, count)
        if kind == 0:
            x_tile(i, n % SLOTS)
        else:
            m_tile(kind - 1, i, n % SLOTS)
        for f, args in hooks.get(n, ()):
            f(*args)

    for d in range(N - 1):
        mucopy(d).wait_recv()
    total = mbuf[0]
    for i in range(1, N):
        total = total + mbuf[i]
    scalar = WARMTH + coef * jnp.sum(total, axis=1, keepdims=True)
    racc[0] = acc[0, at_row(r)] + xin[z]
    racc[1] = acc[1, at_row(r)]
    for d in range(R - 1):
        mcopy(d, 0).wait_recv()
        racc[0] = racc[0] + mrecv[d, 0]
    for d in range(R - 1):
        @pl.when(z <= lax.rem(r - d - 1 + R, R))
        def _():
            mcopy(d, 1).wait_recv()
            racc[1] = racc[1] + mrecv[d, 1]

    cn = c_in[...] + STEP * (coef * racc[0] - scalar * c_in[...])
    rn = r_in[...] + STEP * (coef * racc[1] - scalar * r_in[...])
    csrc[0] = cn
    c_full[at_row(r)] = cn
    fulls = [c_full]
    if last:
        csrc[1] = rn
        r_full[at_row(r)] = rn
        fulls.append(r_full)
    else:
        c_out[...] = cn
        r_out[...] = rn

    def gcopy(d, which):
        return rc(csrc.at[which], fulls[which].at[at_row(r)], cs.at[d, which], crs.at[d, which], rows[d], c)

    for which in range(len(fulls)):
        for d in range(R - 1):
            gcopy(d, which).start()
    for d in range(N - 1):
        mucopy(d).wait_send()
    for p in range(Z):
        @pl.when(jnp.logical_and(p <= z, z < Z - 1))
        def _():
            flow(p, 2).wait_send()

        @pl.when(jnp.logical_and(p >= z, z > 0))
        def _():
            flow(p, -2).wait_send()
    for d in range(R - 1):
        inplane(d, rows[d]).wait_send()
        mcopy(d, 0).wait_send()

    @pl.when(low)
    def _():
        for d in range(R - 1):
            mcopy(d, 1).wait_send()
            xcopy2(d).wait_send()
    for j in range(Z):
        @pl.when(z < j)
        def _():
            upcopy(j, c + 2).wait_send()
    for which in range(len(fulls)):
        for d in range(R - 1):
            gcopy(d, which).wait()


def block_call(last, coef, R, Z, hc, hr, c_full, c, r):
    dma, vmem = pltpu.SemaphoreType.DMA, pltpu.VMEM
    T, U = c.shape
    M, N, CH = R * T, 2 * Z, U // 4
    scratch = [
        vmem((SLOTS, CH, U), F32),
        vmem((M, 2 * U), F32),
        vmem((2, M, U), F32),
        vmem((M, 2 * U), F32),
        vmem((2 * M, 2 * U), BF16),
        vmem((2 * M, U), BF16),
        vmem((M, U), F32),
        vmem((M, U), F32),
        vmem((R, T, U), F32),
        vmem((Z, T, U), F32),
        vmem((R - 1, 2, T, U), F32),
        vmem((2, T, U), F32),
        vmem((2, T, U), F32),
        vmem((Z, T, U), F32),
        vmem((N, T, 128), F32),
        dma((SLOTS,)),
    ]
    scratch += [dma, dma, dma((R - 1,)), dma((R - 1,)), dma((Z,)), dma((Z,))] + [dma((R - 1, 2))] * 4
    scratch += [dma((Z,))] * 4 + [dma((R - 1,))] * 2 + [dma, dma] + [dma((N - 1,))] * 2
    piece, full = (T, U), (M, U)
    shapes = (full, full) if last else (piece, piece, full)
    spec, hbm = pl.BlockSpec(memory_space=pltpu.VMEM), pl.BlockSpec(memory_space=pl.ANY)
    return pl.pallas_call(
        functools.partial(block_kernel, last, coef, R, Z),
        out_shape=[jax.ShapeDtypeStruct(s, F32) for s in shapes],
        in_specs=[hbm, hbm, spec, spec, spec],
        out_specs=[spec] * len(shapes),
        scratch_shapes=scratch,
        name="block_last" if last else "block_mid",
        compiler_params=pltpu.CompilerParams(collective_id=2 if last else 1, has_side_effects=True),
    )(hc, hr, c_full, c, r)


def kernel_body(hist_corr, hist_resp, row_corr, row_resp):
    R, N = lax.axis_size("row"), lax.axis_size("col")
    T = row_corr.shape[0] // R
    coef = 1.0 / math.sqrt(hist_corr.shape[0] * R)
    start = lax.axis_index("row") * T
    corr = lax.dynamic_slice_in_dim(row_corr, start, T, 0)
    resp = lax.dynamic_slice_in_dim(row_resp, start, T, 0)
    full = row_corr
    for _ in range(BLOCKS - 1):
        corr, resp, full = block_call(False, coef, R, N // 2, hist_corr, hist_resp, full, corr, resp)
    return tuple(block_call(True, coef, R, N // 2, hist_corr, hist_resp, full, corr, resp))


def solution(mesh):
    R, N = mesh.shape["row"], mesh.shape["col"]
    body = kernel_body if N == 2 * R and R == 4 else plain_body
    in_specs = (P("row", "col"), P("row", "col"), P(None, "col"), P(None, "col"))
    out_specs = (P(None, "col"), P(None, "col"))
    return jax.shard_map(body, mesh=mesh, in_specs=in_specs, out_specs=out_specs, check_vma=False)
```

profile of v0, /device:TPU:0, one launch (start us, length us, event | category | flops | bytes accessed | tf_op | source)
XLA Modules:
  0.0 473.8 jit_solution(9966456010261852153)
XLA Ops:
  0.6 1.9 constant_dynamic-slice_fusion
  2.5 108.8 %block_mid.3 = (f32[32,2048]{1,0:T(8,128)}, f32[32,2048]{1,0:T(8,128)}, f32[128,2048]{1,0:T(8,128)}) custom-call(f32[4096,2048]{1,0:T(8,128)} %hc.7, f32[4096,2048]{1,0:T(8,128)} %hr.7, f32[128,2048]{1,0:T(8,128)} %c_prev.1, f32[32,2048]{1,0:T(8,128)} %get-tuple-element.21.c_in, f32[32,2048]{1,0:T(8,128)} %get-tuple-element.20.r_in), custom_call_target="tpu_custom_call" | custom-call | tf_op jit(solution)/shard_map/block_mid/pallas_call | solution.py:412
  111.3 115.4 %block_mid.4 = (f32[32,2048]{1,0:T(8,128)}, f32[32,2048]{1,0:T(8,128)}, f32[128,2048]{1,0:T(8,128)}) custom-call(f32[4096,2048]{1,0:T(8,128)} %hc.7, f32[4096,2048]{1,0:T(8,128)} %hr.7, f32[128,2048]{1,0:T(8,128)} %get-tuple-element.11.c_prev, f32[32,2048]{1,0:T(8,128)} %get-tuple-element.12.c_in, f32[32,2048]{1,0:T(8,128)} %get-tuple-element.13.r_in), custom_call_target="tpu_custom_call" | custom-call | tf_op jit(solution)/shard_map/block_mid/pallas_call | solution.py:412
  226.7 115.7 %block_mid.5 = (f32[32,2048]{1,0:T(8,128)}, f32[32,2048]{1,0:T(8,128)}, f32[128,2048]{1,0:T(8,128)}) custom-call(f32[4096,2048]{1,0:T(8,128)} %hc.7, f32[4096,2048]{1,0:T(8,128)} %hr.7, f32[128,2048]{1,0:T(8,128)} %get-tuple-element.14.c_prev, f32[32,2048]{1,0:T(8,128)} %get-tuple-element.15.c_in, f32[32,2048]{1,0:T(8,128)} %get-tuple-element.16.r_in), custom_call_target="tpu_custom_call" | custom-call | tf_op jit(solution)/shard_map/block_mid/pallas_call | solution.py:412
  342.4 126.8 %block_last.1 = (f32[128,2048]{1,0:T(8,128)}, f32[128,2048]{1,0:T(8,128)}) custom-call(f32[4096,2048]{1,0:T(8,128)} %hc.7, f32[4096,2048]{1,0:T(8,128)} %hr.7, f32[128,2048]{1,0:T(8,128)} %get-tuple-element.17.c_prev, f32[32,2048]{1,0:T(8,128)} %get-tuple-element.18.c_in, f32[32,2048]{1,0:T(8,128)} %get-tuple-element.19.r_in), custom_call_target="tpu_custom_call" | custom-call | tf_op jit(solution)/shard_map/block_last/pallas_call | solution.py:412
  469.2 2.3 copy.8
  471.5 2.3 copy.9
where the time goes:
time: 483 us; the launch traced here: 474 us
  Pallas kernels  467 us (97%)
  local copies, waits for them, and re-layouts  6.45 us (1%)
    pallas_call x4, Pallas kernels, block_call(): pl.pallas_call(functools.partial(block_kernel, last, coef, R, Z), out_sha...  467 us

commit v1 on v0

v1 whole, which is shorter than its diff:
```python
import functools
import math

import jax
import jax.numpy as jnp
from jax import lax
from jax.experimental import pallas as pl
from jax.experimental.pallas import tpu as pltpu
from jax.sharding import PartitionSpec as P

BLOCKS = 4
STEP = 0.2
WARMTH = 0.6


def plain_body(hist_corr, hist_resp, row_corr, row_resp):
    rows = lax.axis_size("row")
    span = row_corr.shape[0] // rows
    coef = 1.0 / math.sqrt(hist_corr.shape[0] * rows)
    start = lax.axis_index("row") * span
    corr = lax.dynamic_slice_in_dim(row_corr, start, span, 0)
    resp = lax.dynamic_slice_in_dim(row_resp, start, span, 0)

    def dot(a, b, dims):
        return lax.dot_general(
            a, b, (dims, ((), ())), precision=lax.Precision.HIGH, preferred_element_type=jnp.float32
        )

    for _ in range(BLOCKS):
        energy = 3.0 * corr * resp
        slope = 1.5 * corr * corr
        mult = lax.psum(jnp.sum(energy * corr + slope * resp, axis=1), "col")
        full = lax.all_gather(corr, "row", axis=0, tiled=True)
        wide = lax.all_gather(energy, "col", axis=1, tiled=True)
        energy_rows = lax.all_to_all(wide, "row", split_axis=1, concat_axis=0, tiled=True)
        part_cross = dot(1.5 * full * full, hist_resp, ((1,), (1,)))
        turned = lax.all_to_all(part_cross, "row", split_axis=0, concat_axis=1, tiled=True)
        cross = lax.psum_scatter(turned, "col", scatter_dimension=1, tiled=True)
        part_corr = dot(energy_rows, hist_corr, ((1,), (0,)))
        part_resp = dot(energy_rows, hist_resp, ((1,), (0,)))
        mem_corr = lax.psum_scatter(part_corr, "row", scatter_dimension=0, tiled=True)
        mem_resp = lax.psum_scatter(part_resp, "row", scatter_dimension=0, tiled=True)
        scalar = WARMTH + coef * mult[:, None]
        next_corr = corr + STEP * (coef * (mem_corr + cross) - scalar * corr)
        resp = resp + STEP * (coef * mem_resp - scalar * resp)
        corr = next_corr
    return (
        lax.all_gather(corr, "row", axis=0, tiled=True),
        lax.all_gather(resp, "row", axis=0, tiled=True),
    )


MESH = pl.DeviceIdType.MESH
F32 = jnp.float32


BF16 = jnp.bfloat16
F8 = jnp.float8_e4m3fn
SCALE = 131072.0
STAGES = 4
PIECE = 128
CH = 512
NN = (((1,), (0,)), ((), ()))
NT = (((1,), (1,)), ((), ()))


def split(x):
    hi = x.astype(BF16)
    return hi, (x - hi.astype(F32)).astype(BF16)


def dot(a, b, dims):
    return lax.dot_general(a, b, dims, preferred_element_type=F32)


def blocks_kernel(coef, R, Z, hc, hr, c0, r0, c_full, r_full, lo_hbm, *refs):
    refs = list(refs)
    take = lambda n: [refs.pop(0) for _ in range(n)]
    hchi, hrhi, hrlo, ring, stage = take(5)
    c_st, r_st, racc, dstack, estack, W = take(6)
    xown, xbuf, up, eall, mrecv, mbuf = take(6)
    bar, isem, ssem, lsem, osem = take(5)
    xs, xr, us, ur, ms, mrs, cs, crs = take(8)
    eus, eur, eds, edr, eis, eir, ps, pr, mus, mur = take(10)
    assert not refs
    T, U = c_st.shape
    M = R * T
    N = 2 * Z
    S = hc.shape[0]
    per = U // CH
    K = S // 4
    r, c = lax.axis_index("row"), lax.axis_index("col")
    z = lax.div(c, 2)
    k = c - 2 * z
    partner = 2 * z + 1 - k
    rows = [lax.rem(r + d, R) for d in range(1, R)]
    cols = [lax.rem(c + d, N) for d in range(1, N)]
    low = z <= r

    def rc(src, dst, ss, rs, row, col):
        return pltpu.make_async_remote_copy(
            src_ref=src, dst_ref=dst, send_sem=ss, recv_sem=rs, device_id=(row, col), device_id_type=MESH
        )

    def at_row(q):
        return pl.ds(pl.multiple_of(q * T, T), T)

    def half(h):
        return pl.ds(pl.multiple_of(h * U, U), U)

    def chunk(i, base=0):
        return pl.ds(base + i * CH, CH)

    pieces = S // PIECE
    group = CH // PIECE

    def x_row(t):
        side = jnp.where(lax.rem(t, 2) == 0, 1 - k, k)
        return side * U + lax.div(t, 2) * CH

    def piece_row(n):
        return pl.multiple_of(x_row(lax.div(n, group)) + lax.rem(n, group) * PIECE, PIECE)

    def piece_copy(src, start, n):
        slot = lax.rem(n, STAGES)
        return pltpu.make_async_copy(src.at[pl.ds(start, PIECE)], stage.at[slot], ssem.at[slot])

    def piece_start(n):
        @pl.when(n < pieces)
        def _():
            piece_copy(hr, piece_row(n), n).start()

        @pl.when(jnp.logical_and(n >= pieces, n < 2 * pieces))
        def _():
            piece_copy(hc, pl.multiple_of((n - pieces) * PIECE, PIECE), n).start()

    def piece_split(n, hi_ref, row, lo_ref, lo_row):
        slot = lax.rem(n, STAGES)
        piece_copy(hc, 0, n).wait()

        @pl.loop(0, PIECE // 32)
        def _(i):
            x = stage[slot, pl.ds(pl.multiple_of(i * 32, 32), 32), :]
            hi = x.astype(BF16)
            hi_ref[pl.ds(pl.multiple_of(row + i * 32, 32), 32), :] = hi
            lo_ref[pl.ds(pl.multiple_of(lo_row + i * 32, 32), 32), :] = ((x - hi.astype(F32)) * SCALE).astype(F8)

        piece_start(n + STAGES)

    for n in range(STAGES):
        piece_start(jnp.int32(n))
    inits = [
        pltpu.make_async_copy(c0, c_full, isem.at[0]),
        pltpu.make_async_copy(c0.at[at_row(r)], c_st, isem.at[1]),
        pltpu.make_async_copy(r0.at[at_row(r)], r_st, isem.at[2]),
    ]
    for cp in inits:
        cp.start()
    barrier = pltpu.get_barrier_semaphore()

    def greet(sem):
        for q in rows:
            pl.semaphore_signal(sem, inc=1, device_id=(q, c), device_id_type=MESH)
        for q in cols:
            pl.semaphore_signal(sem, inc=1, device_id=(r, q), device_id_type=MESH)

    greet(barrier)
    for cp in inits:
        cp.wait()
    pl.semaphore_wait(barrier, R - 1 + N - 1)

    def flow(p, step):
        ss, rs = (eus, eur) if step > 0 else (eds, edr)
        return rc(eall.at[p], eall.at[p], ss.at[p], rs.at[p], r, c + step)

    def inplane(d, p):
        return rc(eall.at[p], W.at[at_row(r), half(k)], eis.at[d], eir.at[d], p, c)

    def turn(p):
        @pl.when(p == r)
        def _():
            W[at_row(r), half(k)] = eall[p]

        @pl.when(p != r)
        def _():
            inplane(lax.rem(p - r + R, R) - 1, p).start()

    pair = rc(W.at[:, half(k)], W.at[:, half(k)], ps, pr, r, partner)

    def share(h):
        @pl.when(jnp.logical_or(z - r == h, r - z == h))
        def _():
            for d in range(R - 1):
                inplane(d, rows[d]).wait_recv()
            pair.start()

    def hop(h):
        @pl.when(z - h >= 0)
        def _():
            flow(z - h, 2).wait_recv()

            @pl.when(z < Z - 1)
            def _():
                flow(z - h, 2).start()

        @pl.when(z + h <= Z - 1)
        def _():
            flow(z + h, -2).wait_recv()

            @pl.when(z > 0)
            def _():
                flow(z + h, -2).start()

            turn(z + h)

        @pl.when(z - h >= 0)
        def _():
            turn(z - h)

        share(h - 1)

    def mucopy(d):
        return rc(mbuf.at[c], mbuf.at[c], mus.at[d], mur.at[d], r, cols[d])

    def xcopy(i):
        return rc(c_full.at[:, chunk(i)], xbuf.at[:, chunk(i)], xs.at[i], xr.at[i], r, partner)

    def upcopy(i, col):
        return rc(xown.at[:, chunk(i)], up.at[:, chunk(i)], us.at[i], ur.at[i], r, col)

    def mcopy(d, which, i):
        q = rows[d]
        return rc(
            W.at[at_row(q), chunk(i, which * U)],
            mrecv.at[d, which, :, chunk(i)],
            ms.at[d, which, i],
            mrs.at[d, which, i],
            q,
            c,
        )

    def gcopy(d, which):
        src, dst = (c_st, c_full) if which == 0 else (r_st, r_full)
        return rc(src, dst.at[at_row(r)], cs.at[d, which], crs.at[d, which], rows[d], c)

    def climb(zz, i):
        @pl.when(jnp.logical_and(z == zz, low))
        def _():
            xcopy(i).wait()
            both = xown[:, chunk(i)] + xbuf[:, chunk(i)]
            if zz > 0:
                upcopy(i, c).wait_recv()
                both = both + up[:, chunk(i)]
            xown[:, chunk(i)] = both
            if zz < Z - 1:
                @pl.when(z < r)
                def _():
                    upcopy(i, c + 2).start()

    def stack(dst_ref, i, x):
        hi, lo = split(x)
        dst_ref[pl.ds(pl.multiple_of(i * 32, 32), 32), :] = hi
        dst_ref[pl.ds(pl.multiple_of(M + i * 32, 32), 32), :] = lo

    def e_ready():
        share(Z - 1)
        pair.wait()

        @pl.loop(0, M // 32)
        def _(i):
            stack(estack, i, W[pl.ds(pl.multiple_of(i * 32, 32), 32), :])

    def x_tile(b, t):
        @pl.when(b == 0)
        def _():
            @pl.loop(0, group)
            def _(g):
                n = t * group + g
                row = piece_row(n)
                piece_split(n, hrhi, row, hrlo, row)

        @pl.when(low)
        def _():
            out = c_full if t % 2 == 0 else xown
            where = chunk(t // 2)
            start = pl.multiple_of(x_row(jnp.int32(t)), CH)
            out[:, where] = jnp.zeros((M, CH), F32)

            @pl.loop(0, per)
            def _(j):
                at = pl.ds(pl.multiple_of(j * CH, CH), CH)
                both = dstack[:, at]
                p = dot(both, hrhi[pl.ds(start, CH), at], NT)
                q = dot(both[:M], hrlo[pl.ds(start, CH), at].astype(BF16), NT)
                out[:, where] += p[:M] + p[M:] + q * (1.0 / SCALE)

            if t % 2 == 0:
                xcopy(t // 2).start()

    def resp_tile(i):
        @pl.when(low)
        def _():
            where = chunk(i, U)
            W[:, where] = jnp.zeros((M, CH), F32)

            @pl.loop(0, S // CH)
            def _(j):
                at = pl.ds(pl.multiple_of(j * CH, CH), CH)
                both = estack[:, at]
                p = dot(both, hrhi[at, chunk(i)], NN)
                q = dot(both[:M], hrlo[at, chunk(i)].astype(BF16), NN)
                W[:, where] += p[:M] + p[M:] + q * (1.0 / SCALE)

            for d in range(R - 1):
                mcopy(d, 1, i).start()

    def lo_in(j):
        return pltpu.make_async_copy(lo_hbm.at[pl.ds(j * K, K)], ring.at[j % 2], lsem.at[j % 2])

    def lo_out(j):
        return pltpu.make_async_copy(ring.at[j % 2], lo_hbm.at[pl.ds(j * K, K)], osem.at[j % 2])

    def corr_part(b, j):
        @pl.when(b == 0)
        def _():
            if j >= 2:
                lo_out(j - 2).wait()

            @pl.loop(0, K // PIECE)
            def _(g):
                n = pieces + j * (K // PIECE) + g
                piece_split(n, hchi, j * K + g * PIECE, ring.at[j % 2], g * PIECE)

            lo_out(j).start()

        @pl.when(b > 0)
        def _():
            lo_in(j).wait()

        @pl.loop(0, per)
        def _(i):
            at = pl.ds(pl.multiple_of(i * CH, CH), CH)
            both = estack[:, j * K : (j + 1) * K]
            p = dot(both, hchi[j * K : (j + 1) * K, at], NN)
            q = dot(both[:M], ring[j % 2, :, at].astype(BF16), NN)
            out = p[:M] + p[M:] + q * (1.0 / SCALE)
            if j == 0:
                W[:, at] = out
            else:
                W[:, at] += out

        if j < 2:
            @pl.when(b > 0)
            def _():
                lo_in(j + 2).start()

    @pl.loop(0, BLOCKS)
    def _(b):
        energy = 3.0 * c_st[...] * r_st[...]
        eall[z] = energy
        terms = energy * c_st[...] + 1.5 * c_st[...] * c_st[...] * r_st[...]
        part = terms[:, :128]
        for i in range(1, U // 128):
            part = part + terms[:, i * 128 : (i + 1) * 128]
        mbuf[c] = part

        @pl.when(b > 0)
        def _():
            lo_in(0).start()
            lo_in(1).start()
            pl.semaphore_wait(bar, R - 1 + N - 1)

        @pl.when(z < Z - 1)
        def _():
            flow(z, 2).start()

        @pl.when(z > 0)
        def _():
            flow(z, -2).start()

        turn(z)
        for d in range(N - 1):
            mucopy(d).start()
        hop(1)

        @pl.when(b > 0)
        def _():
            for d in range(R - 1):
                gcopy(d, 0).wait()

        @pl.loop(0, M // 32)
        def _(i):
            old = c_full[pl.ds(pl.multiple_of(i * 32, 32), 32), :]
            stack(dstack, i, 1.5 * old * old)

        hooks = {}

        def hook(n, f, *args):
            hooks.setdefault(n, []).append((f, args))

        hook(1, hop, 2)
        for i in range(per):
            hook(min(2 * i + 2, 7), climb, 0, i)
        hook(6, climb, 1, 0)
        hook(7, hop, 3)
        hook(7, climb, 1, 1)
        hook(7, e_ready)
        for n, zz, i in [(8, 1, 2), (8, 2, 0), (9, 1, 3), (9, 2, 1), (10, 2, 2), (10, 3, 0), (11, 2, 3), (12, 3, 1), (14, 3, 2)]:
            hook(n, climb, zz, i)
        hook(15, climb, 3, 3)
        for n in range(16):
            if n < 8:
                x_tile(b, n)
            elif n < 12:
                resp_tile(n - 8)
            else:
                corr_part(b, n - 12)
            for f, args in hooks.get(n, ()):
                f(*args)

        for i in range(per):
            @pl.when(z == r)
            def _():
                W[:, chunk(i)] += xown[:, chunk(i)]

            for d in range(R - 1):
                mcopy(d, 0, i).start()

        for d in range(N - 1):
            mucopy(d).wait_recv()
        total = mbuf[0]
        for i in range(1, N):
            total = total + mbuf[i]
        scalar = WARMTH + coef * jnp.sum(total, axis=1, keepdims=True)
        racc[...] = jnp.zeros((T, U), F32)

        @pl.when(low)
        def _():
            racc[...] = W[at_row(r), U:]

        for d in range(R - 1):
            @pl.when(z <= lax.rem(r - d - 1 + R, R))
            def _():
                for i in range(per):
                    mcopy(d, 1, i).wait_recv()
                racc[...] += mrecv[d, 1]

        r_st[...] = r_st[...] + STEP * (coef * racc[...] - scalar * r_st[...])

        @pl.when(b == BLOCKS - 1)
        def _():
            r_full[at_row(r), :] = r_st[...]
            for d in range(R - 1):
                gcopy(d, 1).start()

        racc[...] = W[at_row(r), :U]
        for d in range(R - 1):
            for i in range(per):
                mcopy(d, 0, i).wait_recv()
            racc[...] += mrecv[d, 0]
        c_st[...] = c_st[...] + STEP * (coef * racc[...] - scalar * c_st[...])
        c_full[at_row(r), :] = c_st[...]
        for d in range(R - 1):
            gcopy(d, 0).start()

        for d in range(N - 1):
            mucopy(d).wait_send()
        for p in range(Z):
            @pl.when(jnp.logical_and(p <= z, z < Z - 1))
            def _():
                flow(p, 2).wait_send()

            @pl.when(jnp.logical_and(p >= z, z > 0))
            def _():
                flow(p, -2).wait_send()
        for d in range(R - 1):
            inplane(d, rows[d]).wait_send()
            for i in range(per):
                mcopy(d, 0, i).wait_send()

        @pl.when(low)
        def _():
            for d in range(R - 1):
                for i in range(per):
                    mcopy(d, 1, i).wait_send()

        @pl.when(z < r)
        def _():
            for i in range(per):
                upcopy(i, c + 2).wait_send()

        @pl.when(b == 0)
        def _():
            lo_out(2).wait()
            lo_out(3).wait()

        @pl.when(b < BLOCKS - 1)
        def _():
            greet(bar)

    for which in range(2):
        for d in range(R - 1):
            gcopy(d, which).wait()


def kernel_body(hist_corr, hist_resp, row_corr, row_resp):
    R, N = lax.axis_size("row"), lax.axis_size("col")
    Z = N // 2
    M, U = row_corr.shape
    S = hist_corr.shape[0]
    T = M // R
    per = U // CH
    coef = 1.0 / math.sqrt(S * R)
    dma, vmem = pltpu.SemaphoreType.DMA, pltpu.VMEM
    scratch = [
        vmem((S, U), BF16),
        vmem((S, U), BF16),
        vmem((S, U), F8),
        vmem((2, S // 4, U), F8),
        vmem((STAGES, PIECE, U), F32),
        vmem((T, U), F32),
        vmem((T, U), F32),
        vmem((T, U), F32),
        vmem((2 * M, U), BF16),
        vmem((2 * M, 2 * U), BF16),
        vmem((M, 2 * U), F32),
        vmem((M, U), F32),
        vmem((M, U), F32),
        vmem((M, U), F32),
        vmem((Z, T, U), F32),
        vmem((R - 1, 2, T, U), F32),
        vmem((N, T, 128), F32),
        pltpu.SemaphoreType.REGULAR,
        dma((3,)),
        dma((STAGES,)),
        dma((2,)),
        dma((2,)),
    ]
    scratch += [dma((per,))] * 4 + [dma((R - 1, 2, per))] * 2 + [dma((R - 1, 2))] * 2
    scratch += [dma((Z,))] * 4 + [dma((R - 1,))] * 2 + [dma, dma] + [dma((N - 1,))] * 2
    hbm, whole = pl.BlockSpec(memory_space=pl.ANY), pl.BlockSpec(memory_space=pltpu.VMEM)
    full = jax.ShapeDtypeStruct((M, U), F32)
    out = pl.pallas_call(
        functools.partial(blocks_kernel, coef, R, Z),
        out_shape=[full, full, jax.ShapeDtypeStruct((S, U), F8)],
        in_specs=[hbm] * 4,
        out_specs=[whole, whole, hbm],
        scratch_shapes=scratch,
        name="blocks",
        compiler_params=pltpu.CompilerParams(collective_id=1, has_side_effects=True, vmem_limit_bytes=67_043_328),
    )(hist_corr, hist_resp, row_corr, row_resp)
    return tuple(out[:2])


def solution(mesh):
    R, N = mesh.shape["row"], mesh.shape["col"]
    body = kernel_body if N == 2 * R and R == 4 else plain_body
    in_specs = (P("row", "col"), P("row", "col"), P(None, "col"), P(None, "col"))
    out_specs = (P(None, "col"), P(None, "col"))
    return jax.shard_map(body, mesh=mesh, in_specs=in_specs, out_specs=out_specs, check_vma=False)
```

time: 483 us -> 408 us (0.84); the launches traced: 474 us -> 405 us
  Pallas kernels: 467 us -> 400 us
    pallas_call x4 -> x1, Pallas kernels: 467 us -> 400 us  [kernel_body(): pl.pallas_call(functools.partial(blocks_kernel, coef, R, Z), out_shape=[f...]
where the time goes in v1:
time: 408 us; the launch traced here: 405 us
  Pallas kernels  400 us (98%)
  local copies, waits for them, and re-layouts  4.59 us (1%)
    pallas_call x1, Pallas kernels, kernel_body(): pl.pallas_call(functools.partial(blocks_kernel, coef, R, Z), out_shape=[f...  400 us

profile of v1, /device:TPU:0, one launch (start us, length us, event | category | flops | bytes accessed | tf_op | source)
XLA Modules:
  0.0 405.3 jit_solution(5260394944493873088)
XLA Ops:
  0.6 400.0 %blocks.1 = (f32[128,2048]{1,0:T(8,128)}, f32[128,2048]{1,0:T(8,128)}, f8e4m3fn[4096,2048]{1,0:T(8,128)(4,1)}) custom-call(f32[4096,2048]{1,0:T(8,128)} %hc.1, f32[4096,2048]{1,0:T(8,128)} %hr.1, f32[128,2048]{1,0:T(8,128)} %c0.1, f32[128,2048]{1,0:T(8,128)} %r0.1), custom_call_target="tpu_custom_call" | custom-call | tf_op jit(solution)/shard_map/blocks/pallas_call | solution.py:543
  400.7 2.3 copy.8
  403.0 2.3 copy.9

commit v2 on v1

--- a/solution.py
+++ b/solution.py
@@ -60,6 +60,7 @@
 STAGES = 4
 PIECE = 128
 CH = 512
+KX = 1024
 NN = (((1,), (0,)), ((), ()))
 NT = (((1,), (1,)), ((), ()))
 
@@ -84,6 +85,7 @@
     eus, eur, eds, edr, eis, eir, ps, pr, mus, mur = take(10)
     assert not refs
     T, U = c_st.shape
+    H = T // 2
     M = R * T
     N = 2 * Z
     S = hc.shape[0]
@@ -169,55 +171,63 @@
         cp.wait()
     pl.semaphore_wait(barrier, R - 1 + N - 1)
 
-    def flow(p, step):
+    def part(s):
+        return pl.ds(s * H, H)
+
+    def e_rows(q, s):
+        return pl.ds(pl.multiple_of(q * T + s * H, H), H)
+
+    def flow(p, step, s):
         ss, rs = (eus, eur) if step > 0 else (eds, edr)
-        return rc(eall.at[p], eall.at[p], ss.at[p], rs.at[p], r, c + step)
-
-    def inplane(d, p):
-        return rc(eall.at[p], W.at[at_row(r), half(k)], eis.at[d], eir.at[d], p, c)
-
-    def turn(p):
+        return rc(eall.at[p, part(s)], eall.at[p, part(s)], ss.at[p, s], rs.at[p, s], r, c + step)
+
+    def inplane(d, p, s):
+        return rc(eall.at[p, part(s)], W.at[e_rows(r, s), half(k)], eis.at[d, s], eir.at[d, s], p, c)
+
+    def turn(p, s):
         @pl.when(p == r)
         def _():
-            W[at_row(r), half(k)] = eall[p]
+            W[e_rows(r, s), half(k)] = eall[p, part(s)]
 
         @pl.when(p != r)
         def _():
-            inplane(lax.rem(p - r + R, R) - 1, p).start()
-
-    pair = rc(W.at[:, half(k)], W.at[:, half(k)], ps, pr, r, partner)
+            inplane(lax.rem(p - r + R, R) - 1, p, s).start()
+
+    def pair(q):
+        piece = W.at[at_row(q), half(k)]
+        return rc(piece, piece, ps.at[q], pr.at[q], r, partner)
 
     def share(h):
         @pl.when(jnp.logical_or(z - r == h, r - z == h))
         def _():
+            pair(r).start()
             for d in range(R - 1):
-                inplane(d, rows[d]).wait_recv()
-            pair.start()
-
-    def hop(h):
+                for s in range(2):
+                    inplane(d, rows[d], s).wait_recv()
+                pair(lax.rem(r - d - 1 + R, R)).start()
+
+    def hop(h, s):
         @pl.when(z - h >= 0)
         def _():
-            flow(z - h, 2).wait_recv()
+            flow(z - h, 2, s).wait_recv()
 
             @pl.when(z < Z - 1)
             def _():
-                flow(z - h, 2).start()
+                flow(z - h, 2, s).start()
 
         @pl.when(z + h <= Z - 1)
         def _():
-            flow(z + h, -2).wait_recv()
+            flow(z + h, -2, s).wait_recv()
 
             @pl.when(z > 0)
             def _():
-                flow(z + h, -2).start()
-
-            turn(z + h)
+                flow(z + h, -2, s).start()
+
+            turn(z + h, s)
 
         @pl.when(z - h >= 0)
         def _():
-            turn(z - h)
-
-        share(h - 1)
+            turn(z - h, s)
 
     def mucopy(d):
         return rc(mbuf.at[c], mbuf.at[c], mus.at[d], mur.at[d], r, cols[d])
@@ -264,7 +274,8 @@
 
     def e_ready():
         share(Z - 1)
-        pair.wait()
+        for q in range(R):
+            pair(q).wait()
 
         @pl.loop(0, M // 32)
         def _(i):
@@ -286,9 +297,9 @@
             start = pl.multiple_of(x_row(jnp.int32(t)), CH)
             out[:, where] = jnp.zeros((M, CH), F32)
 
-            @pl.loop(0, per)
+            @pl.loop(0, U // KX)
             def _(j):
-                at = pl.ds(pl.multiple_of(j * CH, CH), CH)
+                at = pl.ds(pl.multiple_of(j * KX, KX), KX)
                 both = dstack[:, at]
                 p = dot(both, hrhi[pl.ds(start, CH), at], NT)
                 q = dot(both[:M], hrlo[pl.ds(start, CH), at].astype(BF16), NT)
@@ -303,9 +314,9 @@
             where = chunk(i, U)
             W[:, where] = jnp.zeros((M, CH), F32)
 
-            @pl.loop(0, S // CH)
+            @pl.loop(0, S // K)
             def _(j):
-                at = pl.ds(pl.multiple_of(j * CH, CH), CH)
+                at = pl.ds(pl.multiple_of(j * K, K), K)
                 both = estack[:, at]
                 p = dot(both, hrhi[at, chunk(i)], NN)
                 q = dot(both[:M], hrlo[at, chunk(i)].astype(BF16), NN)
@@ -370,18 +381,22 @@
             lo_in(1).start()
             pl.semaphore_wait(bar, R - 1 + N - 1)
 
-        @pl.when(z < Z - 1)
-        def _():
-            flow(z, 2).start()
-
-        @pl.when(z > 0)
-        def _():
-            flow(z, -2).start()
-
-        turn(z)
+        for s in range(2):
+            @pl.when(z < Z - 1)
+            def _():
+                flow(z, 2, s).start()
+
+            @pl.when(z > 0)
+            def _():
+                flow(z, -2, s).start()
+
+        for s in range(2):
+            turn(z, s)
         for d in range(N - 1):
             mucopy(d).start()
-        hop(1)
+        hop(1, 0)
+        hop(1, 1)
+        hop(2, 0)
 
         @pl.when(b > 0)
         def _():
@@ -398,16 +413,18 @@
         def hook(n, f, *args):
             hooks.setdefault(n, []).append((f, args))
 
-        hook(1, hop, 2)
         for i in range(per):
             hook(min(2 * i + 2, 7), climb, 0, i)
-        hook(6, climb, 1, 0)
-        hook(7, hop, 3)
-        hook(7, climb, 1, 1)
+        hook(1, hop, 3, 1)
+        hook(3, share, 0)
+        hook(5, share, 1)
+        hook(6, share, 2)
+        hook(7, climb, 1, 0)
         hook(7, e_ready)
-        for n, zz, i in [(8, 1, 2), (8, 2, 0), (9, 1, 3), (9, 2, 1), (10, 2, 2), (10, 3, 0), (11, 2, 3), (12, 3, 1), (14, 3, 2)]:
+        for n, zz, i in [(8, 1, 1), (9, 2, 0), (11, 1, 2), (11, 2, 1), (12, 3, 0), (14, 1, 3), (14, 2, 2)]:
             hook(n, climb, zz, i)
-        hook(15, climb, 3, 3)
+        hop(2, 1)
+        hop(3, 0)
         for n in range(16):
             if n < 8:
                 x_tile(b, n)
@@ -419,6 +436,11 @@
                 f(*args)
 
         for i in range(per):
+            if i == per - 1:
+                climb(Z - 2, i)
+            if i >= 1:
+                climb(Z - 1, i)
+
             @pl.when(z == r)
             def _():
                 W[:, chunk(i)] += xown[:, chunk(i)]
@@ -468,13 +490,16 @@
         for p in range(Z):
             @pl.when(jnp.logical_and(p <= z, z < Z - 1))
             def _():
-                flow(p, 2).wait_send()
+                for s in range(2):
+                    flow(p, 2, s).wait_send()
 
             @pl.when(jnp.logical_and(p >= z, z > 0))
             def _():
-                flow(p, -2).wait_send()
+                for s in range(2):
+                    flow(p, -2, s).wait_send()
         for d in range(R - 1):
-            inplane(d, rows[d]).wait_send()
+            for s in range(2):
+                inplane(d, rows[d], s).wait_send()
             for i in range(per):
                 mcopy(d, 0, i).wait_send()
 
@@ -537,7 +562,7 @@
         dma((2,)),
     ]
     scratch += [dma((per,))] * 4 + [dma((R - 1, 2, per))] * 2 + [dma((R - 1, 2))] * 2
-    scratch += [dma((Z,))] * 4 + [dma((R - 1,))] * 2 + [dma, dma] + [dma((N - 1,))] * 2
+    scratch += [dma((Z, 2))] * 4 + [dma((R - 1, 2))] * 2 + [dma((R,))] * 2 + [dma((N - 1,))] * 2
     hbm, whole = pl.BlockSpec(memory_space=pl.ANY), pl.BlockSpec(memory_space=pltpu.VMEM)
     full = jax.ShapeDtypeStruct((M, U), F32)
     out = pl.pallas_call(

time: 408 us -> 326 us (0.80)
  Pallas kernels: 400 us -> 321 us
    pallas_call x1, Pallas kernels: 400 us -> 321 us  [kernel_body(): pl.pallas_call(functools.partial(blocks_kernel, coef, R, Z), out_shape=[f...]
where the time goes in v2:
time: 326 us
  Pallas kernels  321 us (98%)
  local copies, waits for them, and re-layouts  4.59 us (1%)
    pallas_call x1, Pallas kernels, kernel_body(): pl.pallas_call(functools.partial(blocks_kernel, coef, R, Z), out_shape=[f...  321 us

profile of v2, /device:TPU:0, one launch (start us, length us, event | category | flops | bytes accessed | tf_op | source)
XLA Modules:
  0.0 325.8 jit_solution(4503244819399404557)
XLA Ops:
  0.6 320.6 %blocks.1 = (f32[128,2048]{1,0:T(8,128)}, f32[128,2048]{1,0:T(8,128)}, f8e4m3fn[4096,2048]{1,0:T(8,128)(4,1)}) custom-call(f32[4096,2048]{1,0:T(8,128)} %hc.1, f32[4096,2048]{1,0:T(8,128)} %hr.1, f32[128,2048]{1,0:T(8,128)} %c0.1, f32[128,2048]{1,0:T(8,128)} %r0.1), custom_call_target="tpu_custom_call" | custom-call | tf_op jit(solution)/shard_map/blocks/pallas_call | solution.py:568
  321.3 2.3 copy.8
  323.6 2.3 copy.9

commit v3 on v2

--- a/solution.py
+++ b/solution.py
@@ -397,11 +397,14 @@
         hop(1, 0)
         hop(1, 1)
         hop(2, 0)
+        hop(2, 1)
 
         @pl.when(b > 0)
         def _():
             for d in range(R - 1):
                 gcopy(d, 0).wait()
+
+        hop(3, 0)
 
         @pl.loop(0, M // 32)
         def _(i):
@@ -415,7 +418,7 @@
 
         for i in range(per):
             hook(min(2 * i + 2, 7), climb, 0, i)
-        hook(1, hop, 3, 1)
+        hook(0, hop, 3, 1)
         hook(3, share, 0)
         hook(5, share, 1)
         hook(6, share, 2)
@@ -423,8 +426,6 @@
         hook(7, e_ready)
         for n, zz, i in [(8, 1, 1), (9, 2, 0), (11, 1, 2), (11, 2, 1), (12, 3, 0), (14, 1, 3), (14, 2, 2)]:
             hook(n, climb, zz, i)
-        hop(2, 1)
-        hop(3, 0)
         for n in range(16):
             if n < 8:
                 x_tile(b, n)

time: 326 us -> 328 us (level)
  no operation moved by 1% of the time
where the time goes in v3:
time: 328 us
  Pallas kernels  323 us (98%)
  local copies, waits for them, and re-layouts  4.59 us (1%)
    pallas_call x1, Pallas kernels, kernel_body(): pl.pallas_call(functools.partial(blocks_kernel, coef, R, Z), out_shape=[f...  323 us

profile of v3, /device:TPU:0, one launch (start us, length us, event | category | flops | bytes accessed | tf_op | source)
XLA Modules:
  0.0 327.9 jit_solution(12532905301362820701)
XLA Ops:
  0.6 322.6 %blocks.1 = (f32[128,2048]{1,0:T(8,128)}, f32[128,2048]{1,0:T(8,128)}, f8e4m3fn[4096,2048]{1,0:T(8,128)(4,1)}) custom-call(f32[4096,2048]{1,0:T(8,128)} %hc.1, f32[4096,2048]{1,0:T(8,128)} %hr.1, f32[128,2048]{1,0:T(8,128)} %c0.1, f32[128,2048]{1,0:T(8,128)} %r0.1), custom_call_target="tpu_custom_call" | custom-call | tf_op jit(solution)/shard_map/blocks/pallas_call | solution.py:569
  323.3 2.3 copy.8
  325.6 2.3 copy.9
